TPU v7x, 32 devices: a whole 2x2x4 slice. The times are simulated.
32 devices in a mesh: tm: 32 (over z, y, x, core).
Axes of the slice: x: 2, y: 2, z: 4, core: 2. Of those that a mesh axis runs over, the one named last changes fastest.
Arguments:
- wrapped: float32 [4096, 3, 512], P('tm'), may hold values from 0 to 1, as said below
- crossings: int32 [4096, 3, 512], P('tm'), may hold values from -1 to 1, as said below
- box_size: float32 [3], replicated, may hold values from 4 to 12
Outputs:
- msd: float32 [512, 128], P('tm')
Inputs may be any that keep to these rules, and one draw needn't show every extreme that they name: `wrapped`: scaled coordinates within the unit cell. per-frame crossings, one of -1, 0, 1; most entries are 0.
All inputs are finite; a program needn't handle non-finite values.
Results may differ from a plain program's by a relative error of at most 0.0003.
Values sent between devices are 32-bit elements; how exact they have to be, the bound alone decides.
A program may use at most 64 MiB of HBM per device.

v0:
```python
import functools

import jax
import jax.numpy as jnp
from jax import lax
from jax.experimental import pallas as pl
from jax.experimental.pallas import tpu as pltpu
from jax.sharding import PartitionSpec as P

LAGS = 128
LANES = 128
SUB = 8
TURNS = SUB // 2 + 1
MESH = pl.DeviceIdType.MESH


def kernel(n, wrapped, crossings, box, out, wbuf, xbuf, sbuf, hbuf, mean_buf, delta_buf,
           own_ext, far_ext, inner_lag, cross_lag, sq, lagbuf, tbuf, rbuf, load_sem, halo_send, halo_recv, part_send, part_recv):
    dims, groups, frames = wbuf.shape[:3]
    depth = frames // SUB
    per_owner = out.shape[0]
    owners = LANES // per_owner
    me = lax.axis_index("tm")
    is_last = me == n - 1
    prev = lax.rem(me + n - 1, n)
    nxt = lax.rem(me + 1, n)

    barrier = pltpu.get_barrier_semaphore()

    @pl.loop(1, n)
    def _(o):
        pl.semaphore_signal(barrier, inc=1, device_id=(lax.rem(me + o, n),), device_id_type=MESH)

    def load(i, which):
        c, g = i // groups, lax.rem(i, groups)
        lanes = pl.ds(pl.multiple_of(g * LANES, LANES), LANES)
        src, dst = ((wrapped, wbuf), (crossings, xbuf))[which]
        return pltpu.make_async_copy(src.at[c, :, lanes], dst.at[c, g], load_sem.at[which])

    @pl.loop(0, dims * groups)
    def _(i):
        load(i, 0).start()
        load(i, 1).start()

    zero = jnp.zeros((SUB, LANES), jnp.float32)

    @pl.loop(0, groups * TURNS)
    def _(i):
        for d in range(2 * depth):
            inner_lag[i, d] = zero
            cross_lag[i, d] = zero

    @pl.loop(0, groups)
    def _(g):
        for r in range(depth):
            sq[g, r, 0:SUB, :] = zero
            sq[g, r, SUB:2 * SUB, :] = zero

    pltpu.make_async_copy(wbuf, wbuf, load_sem.at[0]).wait()
    pltpu.make_async_copy(xbuf, xbuf, load_sem.at[1]).wait()

    sub_ids = lax.broadcasted_iota(jnp.int32, (SUB, LANES), 0)

    def halo(i):
        return pltpu.make_async_remote_copy(
            src_ref=sbuf.at[i // dims, lax.rem(i, dims)],
            dst_ref=hbuf.at[i // dims, lax.rem(i, dims)],
            send_sem=halo_send, recv_sem=halo_recv.at[i],
            device_id=(prev,), device_id_type=MESH)

    def first_group(device):
        return device * groups // n + 1

    def prepare(step):
        g = lax.rem(step // dims + first_group(prev), groups)
        c = lax.rem(step, dims)
        box_len = box[c]
        counts = [xbuf[c, g, pl.ds(0, SUB, stride=depth), :].astype(jnp.float32)]
        for r in range(1, depth):
            counts.append(counts[-1] + xbuf[c, g, pl.ds(r, SUB, stride=depth), :].astype(jnp.float32))
        incl = counts[-1]
        for shift in (1, 2, 4):
            incl = incl + jnp.where(sub_ids >= shift, pltpu.roll(incl, shift, 0), 0.0)
        total = jnp.broadcast_to(incl[SUB - 1:SUB, :], (SUB, LANES))
        before = incl - counts[-1]
        tot_pos = jnp.zeros((SUB, LANES), jnp.float32)
        for r in range(depth):
            pos = (wbuf[c, g, pl.ds(r, SUB, stride=depth), :] + (counts[r] + before)) * box_len
            sbuf[g, c, r] = pos
            tot_pos = tot_pos + pos
        mean = jnp.broadcast_to(jnp.sum(tot_pos, axis=0, keepdims=True), (SUB, LANES)) * (1.0 / frames)
        mean_buf[g, c] = mean
        delta_buf[g, c] = total * box_len - mean
        return g * dims + c

    def correlate(near, far, buf, row, offsets):
        acc = {}
        for m in range(depth):
            moved = far(m)
            for r in range(depth):
                d = m - r
                if d in offsets:
                    term = moved * near[r]
                    acc[d] = acc[d] + term if d in acc else term
                    if m == depth - 1 or r == depth - 1:
                        buf[row, d + depth - 1] = buf[row, d + depth - 1] + acc[d]

    everything = range(1 - depth, depth)

    def inner(step):
        g = lax.rem(step // dims + first_group(me), groups)
        c = lax.rem(step, dims)
        mean = mean_buf[g, c]
        for r in range(depth):
            own = sbuf[g, c, r] - mean
            own_ext[g, c, r, 0:SUB, :] = own
            own_ext[g, c, r, SUB:2 * SUB, :] = own
            sq[g, r, 0:SUB, :] = sq[g, r, 0:SUB, :] + own * own
        near = [own_ext[g, c, r, 0:SUB, :] * -2.0 for r in range(depth)]
        correlate(near, lambda m: own_ext[g, c, m, 0:SUB, :], inner_lag, g * TURNS, range(depth))

        @pl.loop(1, TURNS)
        def _(q):
            near = [own_ext[g, c, r, 0:SUB, :] * -2.0 for r in range(depth)]
            correlate(near, lambda m: own_ext[g, c, m, pl.ds(q, SUB), :], inner_lag, g * TURNS + q, everything)

    def cross(g, c):
        delta = delta_buf[g, c]
        for r in range(depth):
            far = hbuf[g, c, r] + delta
            far_ext[r, 0:SUB, :] = far
            far_ext[r, SUB:2 * SUB, :] = far
            sq[g, r, SUB:2 * SUB, :] = sq[g, r, SUB:2 * SUB, :] + far * far
        near = [own_ext[g, c, r, 0:SUB, :] * -2.0 for r in range(depth)]
        correlate(near, lambda m: far_ext[m, 0:SUB, :], cross_lag, g * TURNS, range(1 - depth, 0))

        @pl.loop(1, TURNS)
        def _(q):
            low = sub_ids < SUB - q
            near = [jnp.where(low, own_ext[g, c, r, pl.ds(q, SUB), :], own_ext[g, c, r, 0:SUB, :]) * -2.0
                    for r in range(depth)]
            correlate(near, lambda m: jnp.where(low, far_ext[m, 0:SUB, :], far_ext[m, pl.ds(q, SUB), :]),
                      cross_lag, g * TURNS + q, everything)

    @pl.loop(0, groups * dims)
    def _(step):
        prepare(step)

    ahead = groups * dims // 3

    @pl.loop(0, ahead)
    def _(step):
        inner(step)

    pl.semaphore_wait(barrier, n - 1)

    @pl.when(me > 0)
    def _():
        @pl.loop(0, groups * dims)
        def _(step):
            halo(lax.rem(step // dims + first_group(prev), groups) * dims + lax.rem(step, dims)).start()

    @pl.loop(ahead, groups * dims)
    def _(step):
        inner(step)

    end_row = jnp.where(is_last, SUB, 4 * SUB)

    def part(g, d):
        owner = g * owners + d
        return owner, pltpu.make_async_remote_copy(
            src_ref=tbuf.at[owner], dst_ref=rbuf.at[me],
            send_sem=part_send, recv_sem=part_recv,
            device_id=(owner,), device_id_type=MESH)

    @pl.loop(0, groups)
    def _(gi):
        g = lax.rem(gi + first_group(me), groups)

        @pl.when(jnp.logical_not(is_last))
        def _():
            @pl.loop(0, dims)
            def _(c):
                halo(g * dims + c).wait_recv()
                cross(g, c)

        def ins(q, d):
            return inner_lag[g * TURNS + q, d + depth - 1]

        def crs(q, d):
            return cross_lag[g * TURNS + q, d + depth - 1]

        half = SUB // 2
        lows = [sub_ids < SUB - q for q in range(TURNS)]
        for k in range(LAGS):
            q, j = k // depth, k % depth
            if q == 0:
                val = ins(0, j)
            elif q <= half:
                val = jnp.where(lows[q], ins(q, j), crs(q, j))
            else:
                val = jnp.where(lows[SUB - q], crs(SUB - q, j), ins(SUB - q, -j))
            if j > 0:
                if q < half:
                    val = val + jnp.where(lows[q + 1], ins(q + 1, j - depth), crs(q + 1, j - depth))
                elif q < SUB - 1:
                    p = SUB - 1 - q
                    val = val + jnp.where(lows[p], crs(p, j - depth), ins(p, depth - j))
                else:
                    val = val + crs(0, j - depth)
            lagbuf[k * SUB:(k + 1) * SUB, :] = val

        own_total = sq[g, 0, 0:SUB, :]
        for r in range(1, depth):
            own_total = own_total + sq[g, r, 0:SUB, :]

        @pl.loop(0, LAGS // depth)
        def _(q):
            row = sub_ids + q
            near_sum = own_total
            far_sum = sq[g, 0, pl.ds(q, SUB), :]
            for r in range(1, depth):
                far_sum = far_sum + sq[g, r, pl.ds(q, SUB), :]
            for j in range(depth):
                base = jnp.where(row >= end_row, 0.0, jnp.where(row == end_row - 1, near_sum, own_total))
                rows = pl.ds(pl.multiple_of((q * depth + j) * SUB, SUB), SUB)
                lagbuf[rows, :] = lagbuf[rows, :] + (base + far_sum)
                if j < depth - 1:
                    near_sum = near_sum - sq[g, depth - 1 - j, 0:SUB, :]
                    far_sum = far_sum + (sq[g, j, pl.ds(q + 1, SUB), :] - sq[g, j, pl.ds(q, SUB), :])

        blocks = []
        for kb in range(LAGS // SUB):
            val = lagbuf[pl.ds(kb * SUB * SUB, SUB, stride=SUB), :]
            for s in range(1, SUB):
                val = val + lagbuf[pl.ds(kb * SUB * SUB + s, SUB, stride=SUB), :]
            blocks.append(val)
        by_atom = jnp.concatenate(blocks, axis=0).T
        for d in range(owners):
            tbuf[g * owners + d] = by_atom[d * per_owner:(d + 1) * per_owner, :]

        @pl.loop(0, owners)
        def _(d):
            owner, copy = part(g, d)

            @pl.when(owner != me)
            def _():
                copy.start()

    rbuf[me] = tbuf[me]
    others = pl.ds(0, n - 1)
    pltpu.make_async_remote_copy(
        src_ref=tbuf.at[others], dst_ref=rbuf.at[others], send_sem=part_send, recv_sem=part_recv,
        device_id=(nxt,), device_id_type=MESH).wait()
    out[...] = jnp.sum(rbuf[...], axis=0)

    @pl.when(me > 0)
    def _():
        pltpu.make_async_remote_copy(
            src_ref=sbuf, dst_ref=hbuf, send_sem=halo_send, recv_sem=halo_recv.at[0],
            device_id=(prev,), device_id_type=MESH).wait_send()


def on_device(n, wrapped, crossings, box_size):
    frames, dims, atoms = wrapped.shape
    depth, groups = frames // SUB, atoms // LANES
    per_owner = atoms // n
    assert frames == LAGS and atoms % LANES == 0 and LANES % per_owner == 0
    any_spec = pl.BlockSpec(memory_space=pl.ANY)
    f32 = jnp.float32
    lag_sum = pl.pallas_call(
        functools.partial(kernel, n),
        out_shape=jax.ShapeDtypeStruct((per_owner, LAGS), f32),
        in_specs=[any_spec, any_spec, pl.BlockSpec(memory_space=pltpu.SMEM)],
        out_specs=pl.BlockSpec(memory_space=pltpu.VMEM),
        scratch_shapes=[
            pltpu.VMEM((dims, groups, frames, LANES), f32),
            pltpu.VMEM((dims, groups, frames, LANES), jnp.int32),
            pltpu.VMEM((groups, dims, depth, SUB, LANES), f32),
            pltpu.VMEM((groups, dims, depth, SUB, LANES), f32),
            pltpu.VMEM((groups, dims, SUB, LANES), f32),
            pltpu.VMEM((groups, dims, SUB, LANES), f32),
            pltpu.VMEM((groups, dims, depth, 2 * SUB, LANES), f32),
            pltpu.VMEM((depth, 2 * SUB, LANES), f32),
            pltpu.VMEM((groups * TURNS, 2 * depth, SUB, LANES), f32),
            pltpu.VMEM((groups * TURNS, 2 * depth, SUB, LANES), f32),
            pltpu.VMEM((groups, depth, 2 * SUB, LANES), f32),
            pltpu.VMEM((LAGS * SUB, LANES), f32),
            pltpu.VMEM((n, per_owner, LAGS), f32),
            pltpu.VMEM((n, per_owner, LAGS), f32),
            pltpu.SemaphoreType.DMA((2,)),
            pltpu.SemaphoreType.DMA,
            pltpu.SemaphoreType.DMA((groups * dims,)),
            pltpu.SemaphoreType.DMA,
            pltpu.SemaphoreType.DMA,
        ],
        compiler_params=pltpu.CompilerParams(collective_id=0, has_side_effects=True),
    )(jnp.transpose(wrapped, (1, 0, 2)), jnp.transpose(crossings, (1, 0, 2)), box_size)
    divisor = (n * frames - jnp.arange(LAGS, dtype=jnp.int32)).astype(f32)
    return lag_sum / divisor[None, :]


def solution(mesh):
    in_specs = (P("tm", None, None), P("tm", None, None), P())
    out_specs = P("tm", None)
    return jax.shard_map(
        functools.partial(on_device, mesh.shape["tm"]), mesh=mesh,
        in_specs=in_specs, out_specs=out_specs, check_vma=False)
```

profile of v0, /device:TPU:0, one launch (start us, length us, event | category | flops | bytes accessed | tf_op | source)
XLA Modules:
  0.0 26.1 jit_solution(12395110985558402134)
XLA Ops:
  0.0 24.8 %shard_map.37 = f32[16,128]{1,0:T(8,128)} custom-call(f32[3,128,512]{2,1,0:T(8,128)} %bitcast.2, s32[3,128,512]{2,1,0:T(8,128)} %bitcast.3, f32[3]{0:T(128)} %box.1), custom_call_target="tpu_custom_call" | custom-call | tf_op jit(solution)/shard_map/pallas_call | solution.py:271
  24.8 1.3 %broadcast_divide_fusion = f32[16,128]{1,0:T(8,128)} fusion(f32[16,128]{1,0:T(8,128)} %shard_map.37, f32[128]{0:T(128)S(1)} %subtract_convert_fusion), kind=kLoop, calls=%fused_computation | loop fusion | flops 2048 | bytes 16896 | tf_op jit(solution)/shard_map/div | solution.py:300
  (1 shorter events, 0.0 us)
where the time goes:
time: 26.3 us; the launch traced here: 26.1 us
  Pallas kernels  24.8 us (94%)
  other arithmetic  1.31 us (5%)
    pallas_call x1, Pallas kernels, on_device(): pl.pallas_call(functools.partial(kernel, n), out_shape=jax.ShapeDtypeStru...  24.8 us
    div x1, other arithmetic, on_device(): return lag_sum / divisor[None, :]  1.3 us

commit v1 on v0

v1 whole, which is shorter than its diff:
```python
import functools

import jax
import jax.numpy as jnp
import numpy as np
from jax import lax
from jax.experimental import pallas as pl
from jax.experimental.pallas import tpu as pltpu
from jax.sharding import PartitionSpec as P

LAGS = 128
LANES = 128
SUB = 8
SLOTS = 4
GROUP = 2 * SLOTS
MESH = pl.DeviceIdType.MESH
F32 = jnp.float32
BF16 = jnp.bfloat16


def split(x):
    hi = x.astype(BF16)
    return hi, (x - hi.astype(F32)).astype(BF16)


def kernel(n, wrapped, crossings, box, fwd_hbm, inv_hbm, out, wbuf, xbuf, sbuf, rbuf, fwd, inv, spec, zbuf,
           first_sq, last_sq, halo_sq, sum_sq, tbuf, part, load_sem, const_sem, send_sem, recv_sem, pass_sem,
           part_send, part_recv):
    dims, frames = wbuf.shape[:2]
    per_owner = out.shape[0]
    planes = n // GROUP
    quads = n // SLOTS
    width = 2 * per_owner
    sub_planes = LANES // (SLOTS * width)
    me = lax.axis_index("tm")
    plane = me // GROUP
    j = me % GROUP
    chip, core = j // 2, j % 2
    quad = 2 * plane + core
    slot = j % SLOTS
    is_last = quad == quads - 1

    def device(q, i):
        return GROUP * (q // 2) + 2 * i + q % 2

    barrier = pltpu.get_barrier_semaphore()

    @pl.loop(1, GROUP)
    def _(o):
        pl.semaphore_signal(barrier, inc=1, device_id=(GROUP * plane + (j + o) % GROUP,), device_id_type=MESH)

    @pl.loop(1, planes)
    def _(o):
        far = GROUP * ((plane + o) % planes) + 2 * chip
        pl.semaphore_signal(barrier, inc=1, device_id=(far,), device_id_type=MESH)
        pl.semaphore_signal(barrier, inc=1, device_id=(far + 1,), device_id_type=MESH)

    def load(c, which):
        src, dst = ((wrapped, wbuf), (crossings, xbuf))[which]
        return pltpu.make_async_copy(src.at[c], dst.at[c], load_sem.at[c, which])

    for c in range(dims):
        load(c, 1).start()
    for c in range(dims):
        load(c, 0).start()
    const_copies = [pltpu.make_async_copy(fwd_hbm, fwd, const_sem.at[0]),
                    pltpu.make_async_copy(inv_hbm, inv, const_sem.at[1])]
    for copy in const_copies:
        copy.start()

    lane = lax.broadcasted_iota(jnp.int32, (SUB, LANES), 1)
    sub = lax.broadcasted_iota(jnp.int32, (SUB, LANES), 0)

    def swap(a, b, dist):
        low = (lane[0:1] & dist) == 0
        return (jnp.where(low, a, pltpu.roll(b, dist, 1)), jnp.where(low, pltpu.roll(a, LANES - dist, 1), b))

    def pack(groups):
        a = list(groups)
        for k in (0, 1):
            a[k], a[k + 2] = swap(a[k], a[k + 2], 2 * width)
        for k in (0, 2):
            a[k], a[k + 1] = swap(a[k], a[k + 1], width)
        return a

    ones = jnp.ones((SUB, frames), BF16)
    tri = (lax.broadcasted_iota(jnp.int32, (frames, frames), 1)
           <= lax.broadcasted_iota(jnp.int32, (frames, frames), 0)).astype(F32).astype(BF16)

    def rows(c):
        start = 0 if c == 0 else SUB + c * frames
        return pl.ds(start, SUB + (c + 1) * frames - start)

    def lanes(g):
        return pl.ds(g * LANES, LANES)

    for c in range(dims):
        load(c, 1).wait()
    totals = [jnp.dot(ones, xbuf[c].astype(F32).astype(BF16), preferred_element_type=F32) for c in range(dims)]
    groups = []
    for g in range(SLOTS):
        t = [v[:, g * LANES:(g + 1) * LANES] for v in totals]
        groups.append(jnp.where(sub == 0, t[0], jnp.where(sub == 1, t[1], t[2])))
    for i, v in enumerate(pack(groups)):
        sbuf[i, 0:SUB, :] = v

    own_quad = 2 * plane + j // SLOTS

    def exchange(c, o):
        i = 2 * ((chip // 2 + o // 2) % 2) + (chip + o) % 2
        dst = device(own_quad, i)
        src, to = sbuf.at[i, rows(c), :], rbuf.at[slot, rows(c), :]
        remote = pltpu.make_async_remote_copy(
            src_ref=src, dst_ref=to, send_sem=send_sem.at[o, c], recv_sem=recv_sem.at[slot, c],
            device_id=(dst,), device_id_type=MESH)
        return dst == me, remote, pltpu.make_async_copy(src, to, recv_sem.at[slot, c])

    for c in range(dims):
        load(c, 0).wait()
        counts = jnp.dot(tri, xbuf[c].astype(F32).astype(BF16), preferred_element_type=F32)
        wbuf[c] = wbuf[c] + counts
        for r in range(0, frames, SUB):
            for i, v in enumerate(pack([wbuf[c, r:r + SUB, lanes(g)] for g in range(SLOTS)])):
                sbuf[i, SUB + c * frames + r:SUB + c * frames + r + SUB, :] = v
        if c == 0:
            pl.semaphore_wait(barrier, GROUP - 1 + 2 * (planes - 1))
        for o in (3, 1, 2):
            exchange(c, o)[1].start()
        mine, remote, local = exchange(c, 0)

        @pl.when(mine)
        def _():
            local.start()

        @pl.when(jnp.logical_not(mine))
        def _():
            remote.start()

    for copy in const_copies:
        copy.wait()

    def arrived(s, c):
        return pltpu.make_async_remote_copy(
            src_ref=sbuf.at[0, rows(c), :], dst_ref=rbuf.at[s, rows(c), :], send_sem=send_sem.at[0, c],
            recv_sem=recv_sem.at[s, c], device_id=(me,), device_id_type=MESH)

    def landed(s, c):
        pltpu.make_async_copy(sbuf.at[0, rows(c), :], rbuf.at[s, rows(c), :], recv_sem.at[s, c]).wait()

    def hand_on(c):
        return pltpu.make_async_remote_copy(
            src_ref=rbuf.at[0, rows(c), :], dst_ref=rbuf.at[SLOTS, rows(c), :], send_sem=pass_sem.at[c],
            recv_sem=recv_sem.at[SLOTS, c], device_id=(device(quad - 1, chip),), device_id_type=MESH)

    bins = LAGS
    half = bins // 2

    def position(s, c, off):
        u = rbuf[s, SUB + c * frames:SUB + (c + 1) * frames, :]
        return u * box[c] + off

    def total(s, c):
        return rbuf[s, c:c + 1, :]

    def transform(x):
        hi, lo = split(x)
        return jnp.dot(fwd[...], jnp.concatenate([hi, lo, hi], axis=0), preferred_element_type=F32)

    offs = {}

    def main(c):
        landed(0, c)

        @pl.when(quad > 0)
        def _():
            hand_on(c).start()

        for s in range(1, SLOTS):
            landed(s, c)
        mid = rbuf[2, SUB + c * frames:SUB + (c + 1) * frames, :]
        ref = jnp.sum(mid, axis=0, keepdims=True) * (-1.0 / frames)
        shift = [ref - total(1, c) - total(0, c), ref - total(1, c), ref, ref + total(2, c)]
        offs[c] = (ref + total(2, c) + total(3, c)) * box[c]
        xs = [position(s, c, shift[s] * box[c]) for s in range(SLOTS)]
        squares = [x * x for x in xs]
        all_sq = (squares[0] + squares[1]) + (squares[2] + squares[3])
        if c == 0:
            first_sq[...] = squares[0]
            last_sq[...] = squares[3]
            sum_sq[...] = all_sq
        else:
            first_sq[...] = first_sq[...] + squares[0]
            last_sq[...] = last_sq[...] + squares[3]
            sum_sq[...] = sum_sq[...] + all_sq
        for s in range(SLOTS):
            spec[c, s] = transform(xs[s])
        for sign, base in ((1, 0), (-1, half)):
            @pl.loop(0, half // SUB)
            def _(r):
                re_rows = pl.ds(pl.multiple_of(base + r * SUB, SUB), SUB)
                im_rows = pl.ds(pl.multiple_of(bins + base + r * SUB, SUB), SUB)
                res = [spec[c, s, re_rows, :] for s in range(SLOTS)]
                ims = [spec[c, s, im_rows, :] for s in range(SLOTS)]
                z_re = z_im = None
                for s in range(SLOTS):
                    if s < SLOTS - 1:
                        y_re = res[s] + ims[s + 1] if sign > 0 else res[s] - ims[s + 1]
                        y_im = ims[s] - res[s + 1] if sign > 0 else ims[s] + res[s + 1]
                        p_re = res[s] * y_re + ims[s] * y_im
                        p_im = res[s] * y_im - ims[s] * y_re
                        z_im = p_im if z_im is None else z_im + p_im
                    else:
                        p_re = res[s] * res[s] + ims[s] * ims[s]
                    z_re = p_re if z_re is None else z_re + p_re
                if c == 0:
                    zbuf[re_rows, :] = z_re
                    zbuf[im_rows, :] = z_im
                else:
                    zbuf[re_rows, :] = zbuf[re_rows, :] + z_re
                    zbuf[im_rows, :] = zbuf[im_rows, :] + z_im

    def halo(c):
        off = offs[c]

        @pl.when(jnp.logical_not(is_last))
        def _():
            landed(SLOTS, c)
            x = position(SLOTS, c, off)
            if c == 0:
                halo_sq[...] = x * x
            else:
                halo_sq[...] = halo_sq[...] + x * x
            spec[c, 0] = transform(x)
            for sign, base in ((1, 0), (-1, half)):
                @pl.loop(0, half // SUB)
                def _(r):
                    re_rows = pl.ds(pl.multiple_of(base + r * SUB, SUB), SUB)
                    im_rows = pl.ds(pl.multiple_of(bins + base + r * SUB, SUB), SUB)
                    x_re, x_im = spec[c, SLOTS - 1, re_rows, :], spec[c, SLOTS - 1, im_rows, :]
                    y_re, y_im = spec[c, 0, im_rows, :], spec[c, 0, re_rows, :]
                    if sign > 0:
                        zbuf[re_rows, :] = zbuf[re_rows, :] + (x_re * y_re - x_im * y_im)
                        zbuf[im_rows, :] = zbuf[im_rows, :] - (x_re * y_im + x_im * y_re)
                    else:
                        zbuf[re_rows, :] = zbuf[re_rows, :] - (x_re * y_re - x_im * y_im)
                        zbuf[im_rows, :] = zbuf[im_rows, :] + (x_re * y_im + x_im * y_re)

    @pl.when(is_last)
    def _():
        halo_sq[...] = jnp.zeros_like(halo_sq)

    main(0)
    main(1)
    halo(0)
    main(2)
    halo(1)
    halo(2)

    z_hi, z_lo = split(zbuf[...])
    w_hi, w_lo = split(halo_sq[...] - first_sq[...])
    v_hi, v_lo = split(jnp.where(is_last, -last_sq[...], 0.0))
    lag_sum = jnp.dot(inv[...], jnp.concatenate([z_hi, z_lo, z_hi, w_hi, w_lo, v_hi, v_lo], axis=0),
                      preferred_element_type=F32)
    lag_sum = lag_sum + 2.0 * jnp.sum(sum_sq[...], axis=0, keepdims=True)
    by_atom = lag_sum.T
    for g in range(SLOTS):
        for p in range(sub_planes):
            for k in range(2):
                first = p * SLOTS * width + g * width + k * per_owner
                tbuf[2 * (g * sub_planes + p) + k] = by_atom[first:first + per_owner, :]

    @pl.loop(0, quads)
    def _(q):
        @pl.when(q != quad)
        def _():
            pltpu.make_async_remote_copy(
                src_ref=tbuf.at[q], dst_ref=part.at[quad], send_sem=part_send, recv_sem=part_recv,
                device_id=(device(q, chip),), device_id_type=MESH).start()

    part[quad] = tbuf[quad]
    others = pl.ds(0, quads - 1)
    pltpu.make_async_remote_copy(
        src_ref=tbuf.at[others], dst_ref=part.at[others], send_sem=part_send, recv_sem=part_recv,
        device_id=((me + 1) % n,), device_id_type=MESH).wait()
    out[...] = jnp.sum(part[...], axis=0)

    for c in range(dims):
        for o in (3, 1, 2):
            exchange(c, o)[1].wait_send()
        mine, remote, local = exchange(c, 0)

        @pl.when(jnp.logical_not(mine))
        def _():
            remote.wait_send()

        @pl.when(quad > 0)
        def _():
            hand_on(c).wait_send()


def tables(frames):
    f = np.concatenate([np.arange(0, LAGS, 2), np.arange(1, LAGS, 2)]) + 0.5
    t = np.arange(frames)
    angle = 2.0 * np.pi * f[:, None] * t[None, :] / (2 * LAGS)
    fwd = np.concatenate([np.cos(angle), -np.sin(angle)], axis=0).astype(np.float32)
    back = (2.0 * np.pi * f[None, :] * np.arange(LAGS)[:, None]) / (2 * LAGS)
    inv = np.concatenate([np.cos(back), -np.sin(back)], axis=1) * (-2.0 / LAGS)
    inv = inv.astype(np.float32)

    def halves(x):
        hi = x.astype(jnp.bfloat16)
        return hi, (x - hi.astype(np.float32)).astype(jnp.bfloat16)

    k = np.arange(LAGS)[:, None]
    low = (t[None, :] < k).astype(jnp.bfloat16)
    high = (t[None, :] >= frames - k).astype(jnp.bfloat16)
    f_hi, f_lo = halves(fwd)
    i_hi, i_lo = halves(inv)
    return (np.concatenate([f_hi, f_hi, f_lo], axis=1),
            np.concatenate([i_hi, i_hi, i_lo, low, low, high, high], axis=1))


def on_device(n, wrapped, crossings, box_size):
    frames, dims, atoms = wrapped.shape
    per_owner = atoms // n
    quads = n // SLOTS
    assert frames == LAGS and atoms == SLOTS * LANES and n % GROUP == 0 and LANES % (GROUP * per_owner) == 0
    fwd, inv = tables(frames)
    any_spec = pl.BlockSpec(memory_space=pl.ANY)
    piece = SUB + dims * frames
    lag_sum = pl.pallas_call(
        functools.partial(kernel, n),
        out_shape=jax.ShapeDtypeStruct((per_owner, LAGS), F32),
        in_specs=[any_spec, any_spec, pl.BlockSpec(memory_space=pltpu.SMEM), any_spec, any_spec],
        out_specs=pl.BlockSpec(memory_space=pltpu.VMEM),
        scratch_shapes=[
            pltpu.VMEM((dims, frames, atoms), F32),
            pltpu.VMEM((dims, frames, atoms), jnp.int32),
            pltpu.VMEM((SLOTS, piece, LANES), F32),
            pltpu.VMEM((SLOTS + 1, piece, LANES), F32),
            pltpu.VMEM(fwd.shape, BF16),
            pltpu.VMEM(inv.shape, BF16),
            pltpu.VMEM((dims, SLOTS, 2 * LAGS, LANES), F32),
            pltpu.VMEM((2 * LAGS, LANES), F32),
            pltpu.VMEM((frames, LANES), F32),
            pltpu.VMEM((frames, LANES), F32),
            pltpu.VMEM((frames, LANES), F32),
            pltpu.VMEM((frames, LANES), F32),
            pltpu.VMEM((quads, per_owner, LAGS), F32),
            pltpu.VMEM((quads, per_owner, LAGS), F32),
            pltpu.SemaphoreType.DMA((dims, 2)),
            pltpu.SemaphoreType.DMA((2,)),
            pltpu.SemaphoreType.DMA((SLOTS, dims)),
            pltpu.SemaphoreType.DMA((SLOTS + 1, dims)),
            pltpu.SemaphoreType.DMA((dims,)),
            pltpu.SemaphoreType.DMA,
            pltpu.SemaphoreType.DMA,
        ],
        compiler_params=pltpu.CompilerParams(collective_id=0, has_side_effects=True),
    )(jnp.transpose(wrapped, (1, 0, 2)), jnp.transpose(crossings, (1, 0, 2)), box_size,
      jnp.asarray(fwd), jnp.asarray(inv))
    divisor = (n * frames - jnp.arange(LAGS, dtype=jnp.int32)).astype(F32)
    return lag_sum / divisor[None, :]


def solution(mesh):
    in_specs = (P("tm", None, None), P("tm", None, None), P())
    out_specs = P("tm", None)
    return jax.shard_map(
        functools.partial(on_device, mesh.shape["tm"]), mesh=mesh,
        in_specs=in_specs, out_specs=out_specs, check_vma=False)
```

time: 26.3 us -> 24.5 us (0.932)
  Pallas kernels: 24.8 us -> 22.7 us
    pallas_call x1, Pallas kernels: 24.8 us -> 22.7 us  [on_device(): pl.pallas_call(functools.partial(kernel, n), out_shape=jax.ShapeDtypeStru...]
where the time goes in v1:
time: 24.5 us; the launch traced here: 24.1 us
  Pallas kernels  22.7 us (93%)
  other arithmetic  1.31 us (5%)
    pallas_call x1, Pallas kernels, on_device(): pl.pallas_call(functools.partial(kernel, n), out_shape=jax.ShapeDtypeStru...  22.7 us
    div x1, other arithmetic, on_device(): return lag_sum / divisor[None, :]  1.3 us

profile of v1, /device:TPU:0, one launch (start us, length us, event | category | flops | bytes accessed | tf_op | source)
XLA Modules:
  0.0 24.1 jit_solution(7456798347686103312)
XLA Ops:
  0.0 22.7 %shard_map.55 = f32[16,128]{1,0:T(8,128)} custom-call(f32[3,128,512]{2,1,0:T(8,128)} %bitcast.2, s32[3,128,512]{2,1,0:T(8,128)} %bitcast.3, f32[3]{0:T(128)} %box.1, bf16[256,384]{1,0:T(8,128)(2,1)} %constant.6.clone.fwd_hbm, bf16[128,1280]{1,0:T(8,128)(2,1)} %constant.7.clone.inv_hbm), custom_call_target="tpu_custom_call" | custom-call | tf_op jit(solution)/shard_map/pallas_call | solution.py:331
  22.8 1.3 %broadcast_divide_fusion = f32[16,128]{1,0:T(8,128)} fusion(f32[16,128]{1,0:T(8,128)} %shard_map.55, f32[128]{0:T(128)S(1)} %subtract_convert_fusion), kind=kLoop, calls=%fused_computation | loop fusion | flops 2048 | bytes 16896 | tf_op jit(solution)/shard_map/div | solution.py:363
  (1 shorter events, 0.0 us)

commit v2 on v1

--- a/solution.py
+++ b/solution.py
@@ -23,9 +23,9 @@
     return hi, (x - hi.astype(F32)).astype(BF16)
 
 
-def kernel(n, wrapped, crossings, box, fwd_hbm, inv_hbm, out, wbuf, xbuf, sbuf, rbuf, fwd, inv, spec, zbuf,
-           first_sq, last_sq, halo_sq, sum_sq, tbuf, part, load_sem, const_sem, send_sem, recv_sem, pass_sem,
-           part_send, part_recv):
+def kernel(n, wrapped, crossings, box_hbm, fwd_hbm, inv_hbm, out, wbuf, xbuf, sbuf, rbuf, fwd, inv, spec, zbuf,
+           first_sq, last_sq, halo_sq, sum_sq, tbuf, part, load_sem, const_sem, box, send_sem, recv_sem, pass_sem,
+           part_send, part_recv, diag_sem, up_sem, down_sem):
     dims, frames = wbuf.shape[:2]
     per_owner = out.shape[0]
     planes = n // GROUP
@@ -43,28 +43,68 @@
     def device(q, i):
         return GROUP * (q // 2) + 2 * i + q % 2
 
+    x, y = chip % 2, chip // 2
+    partner = me + 1 - 2 * core
+
+    def nearby(o, k):
+        return GROUP * plane + 2 * (2 * ((y + o // 2) % 2) + (x + o) % 2) + k
+
+    def signal(sem, dst):
+        pl.semaphore_signal(sem, inc=1, device_id=(dst,), device_id_type=MESH)
+
     barrier = pltpu.get_barrier_semaphore()
-
-    @pl.loop(1, GROUP)
-    def _(o):
-        pl.semaphore_signal(barrier, inc=1, device_id=(GROUP * plane + (j + o) % GROUP,), device_id_type=MESH)
-
-    @pl.loop(1, planes)
-    def _(o):
-        far = GROUP * ((plane + o) % planes) + 2 * chip
-        pl.semaphore_signal(barrier, inc=1, device_id=(far,), device_id_type=MESH)
-        pl.semaphore_signal(barrier, inc=1, device_id=(far + 1,), device_id_type=MESH)
+    below, above = plane > 0, plane < planes - 1
+    signal(barrier, partner)
+    for k in range(2):
+        signal(barrier, nearby(1, k))
+        signal(barrier, nearby(2, k))
+
+    @pl.when(below)
+    def _():
+        for k in range(2):
+            signal(barrier, GROUP * (plane - 1) + 2 * chip + k)
+
+    @pl.when(above)
+    def _():
+        for k in range(2):
+            signal(barrier, GROUP * (plane + 1) + 2 * chip + k)
+
+    greeted = 5 + 2 * jnp.where(below, 1, 0) + 2 * jnp.where(above, 1, 0)
+
+    def spread(first, last):
+        @pl.loop(first, last)
+        def _(r):
+            @pl.when(below)
+            def _():
+                signal(up_sem, me - GROUP)
+
+            @pl.when(above)
+            def _():
+                signal(down_sem, me + GROUP)
+
+            @pl.when(above)
+            def _():
+                pl.semaphore_wait(up_sem, 1)
+
+            @pl.when(below)
+            def _():
+                pl.semaphore_wait(down_sem, 1)
+
+    rounds = max(planes - 2, 0)
 
     def load(c, which):
         src, dst = ((wrapped, wbuf), (crossings, xbuf))[which]
         return pltpu.make_async_copy(src.at[c], dst.at[c], load_sem.at[c, which])
 
-    for c in range(dims):
+    load(0, 1).start()
+    load(0, 0).start()
+    for c in range(1, dims):
         load(c, 1).start()
-    for c in range(dims):
+    for c in range(1, dims):
         load(c, 0).start()
     const_copies = [pltpu.make_async_copy(fwd_hbm, fwd, const_sem.at[0]),
-                    pltpu.make_async_copy(inv_hbm, inv, const_sem.at[1])]
+                    pltpu.make_async_copy(inv_hbm, inv, const_sem.at[1]),
+                    pltpu.make_async_copy(box_hbm, box, const_sem.at[2])]
     for copy in const_copies:
         copy.start()
 
@@ -88,21 +128,13 @@
            <= lax.broadcasted_iota(jnp.int32, (frames, frames), 0)).astype(F32).astype(BF16)
 
     def rows(c):
-        start = 0 if c == 0 else SUB + c * frames
-        return pl.ds(start, SUB + (c + 1) * frames - start)
+        return (pl.ds(0, frames), pl.ds(frames, SUB + frames), pl.ds(SUB + 2 * frames, frames))[c]
+
+    def row0(c):
+        return c * frames + (SUB if c > 0 else 0)
 
     def lanes(g):
         return pl.ds(g * LANES, LANES)
-
-    for c in range(dims):
-        load(c, 1).wait()
-    totals = [jnp.dot(ones, xbuf[c].astype(F32).astype(BF16), preferred_element_type=F32) for c in range(dims)]
-    groups = []
-    for g in range(SLOTS):
-        t = [v[:, g * LANES:(g + 1) * LANES] for v in totals]
-        groups.append(jnp.where(sub == 0, t[0], jnp.where(sub == 1, t[1], t[2])))
-    for i, v in enumerate(pack(groups)):
-        sbuf[i, 0:SUB, :] = v
 
     own_quad = 2 * plane + j // SLOTS
 
@@ -116,16 +148,34 @@
         return dst == me, remote, pltpu.make_async_copy(src, to, recv_sem.at[slot, c])
 
     for c in range(dims):
+        if c == 1:
+            for k in range(1, dims):
+                load(k, 1).wait()
+            totals = [jnp.dot(ones, xbuf[c].astype(F32).astype(BF16), preferred_element_type=F32) for c in range(dims)]
+            groups = []
+            for g in range(SLOTS):
+                t = [v[:, g * LANES:(g + 1) * LANES] for v in totals]
+                groups.append(jnp.where(sub == 0, t[0], jnp.where(sub == 1, t[1], t[2])))
+            for i, v in enumerate(pack(groups)):
+                sbuf[i, frames:frames + SUB, :] = v
+        if c == 0:
+            load(c, 1).wait()
         load(c, 0).wait()
         counts = jnp.dot(tri, xbuf[c].astype(F32).astype(BF16), preferred_element_type=F32)
         wbuf[c] = wbuf[c] + counts
         for r in range(0, frames, SUB):
             for i, v in enumerate(pack([wbuf[c, r:r + SUB, lanes(g)] for g in range(SLOTS)])):
-                sbuf[i, SUB + c * frames + r:SUB + c * frames + r + SUB, :] = v
+                sbuf[i, row0(c) + r:row0(c) + r + SUB, :] = v
         if c == 0:
-            pl.semaphore_wait(barrier, GROUP - 1 + 2 * (planes - 1))
-        for o in (3, 1, 2):
-            exchange(c, o)[1].start()
+            pl.semaphore_wait(barrier, greeted)
+            signal(diag_sem, nearby(1, core))
+
+        exchange(c, 1)[1].start()
+
+        if c == 2:
+            exchange(c, 3)[1].start()
+
+        exchange(c, 2)[1].start()
         mine, remote, local = exchange(c, 0)
 
         @pl.when(mine)
@@ -135,14 +185,14 @@
         @pl.when(jnp.logical_not(mine))
         def _():
             remote.start()
+
+        if c == 1:
+            pl.semaphore_wait(diag_sem, 1)
+            exchange(0, 3)[1].start()
+            exchange(1, 3)[1].start()
 
     for copy in const_copies:
         copy.wait()
-
-    def arrived(s, c):
-        return pltpu.make_async_remote_copy(
-            src_ref=sbuf.at[0, rows(c), :], dst_ref=rbuf.at[s, rows(c), :], send_sem=send_sem.at[0, c],
-            recv_sem=recv_sem.at[s, c], device_id=(me,), device_id_type=MESH)
 
     def landed(s, c):
         pltpu.make_async_copy(sbuf.at[0, rows(c), :], rbuf.at[s, rows(c), :], recv_sem.at[s, c]).wait()
@@ -156,11 +206,11 @@
     half = bins // 2
 
     def position(s, c, off):
-        u = rbuf[s, SUB + c * frames:SUB + (c + 1) * frames, :]
+        u = rbuf[s, row0(c):row0(c) + frames, :]
         return u * box[c] + off
 
     def total(s, c):
-        return rbuf[s, c:c + 1, :]
+        return rbuf[s, frames + c:frames + c + 1, :]
 
     def transform(x):
         hi, lo = split(x)
@@ -168,7 +218,7 @@
 
     offs = {}
 
-    def main(c):
+    def arrive(c):
         landed(0, c)
 
         @pl.when(quad > 0)
@@ -177,7 +227,9 @@
 
         for s in range(1, SLOTS):
             landed(s, c)
-        mid = rbuf[2, SUB + c * frames:SUB + (c + 1) * frames, :]
+
+    def main(c):
+        mid = rbuf[2, row0(c):row0(c) + frames, :]
         ref = jnp.sum(mid, axis=0, keepdims=True) * (-1.0 / frames)
         shift = [ref - total(1, c) - total(0, c), ref - total(1, c), ref, ref + total(2, c)]
         offs[c] = (ref + total(2, c) + total(3, c)) * box[c]
@@ -249,9 +301,13 @@
     def _():
         halo_sq[...] = jnp.zeros_like(halo_sq)
 
+    arrive(0)
+    spread(0, rounds)
+    arrive(1)
     main(0)
     main(1)
     halo(0)
+    arrive(2)
     main(2)
     halo(1)
     halo(2)
@@ -326,12 +382,12 @@
     quads = n // SLOTS
     assert frames == LAGS and atoms == SLOTS * LANES and n % GROUP == 0 and LANES % (GROUP * per_owner) == 0
     fwd, inv = tables(frames)
-    any_spec = pl.BlockSpec(memory_space=pl.ANY)
+    any_spec = pl.BlockSpec(memory_space=pltpu.HBM)
     piece = SUB + dims * frames
     lag_sum = pl.pallas_call(
         functools.partial(kernel, n),
         out_shape=jax.ShapeDtypeStruct((per_owner, LAGS), F32),
-        in_specs=[any_spec, any_spec, pl.BlockSpec(memory_space=pltpu.SMEM), any_spec, any_spec],
+        in_specs=[any_spec] * 5,
         out_specs=pl.BlockSpec(memory_space=pltpu.VMEM),
         scratch_shapes=[
             pltpu.VMEM((dims, frames, atoms), F32),
@@ -349,14 +405,18 @@
             pltpu.VMEM((quads, per_owner, LAGS), F32),
             pltpu.VMEM((quads, per_owner, LAGS), F32),
             pltpu.SemaphoreType.DMA((dims, 2)),
-            pltpu.SemaphoreType.DMA((2,)),
+            pltpu.SemaphoreType.DMA((3,)),
+            pltpu.SMEM((dims,), F32),
             pltpu.SemaphoreType.DMA((SLOTS, dims)),
             pltpu.SemaphoreType.DMA((SLOTS + 1, dims)),
             pltpu.SemaphoreType.DMA((dims,)),
             pltpu.SemaphoreType.DMA,
             pltpu.SemaphoreType.DMA,
+            pltpu.SemaphoreType.REGULAR,
+            pltpu.SemaphoreType.REGULAR,
+            pltpu.SemaphoreType.REGULAR,
         ],
-        compiler_params=pltpu.CompilerParams(collective_id=0, has_side_effects=True),
+        compiler_params=pltpu.CompilerParams(collective_id=0, has_side_effects=True, vmem_limit_bytes=55200*1024),
     )(jnp.transpose(wrapped, (1, 0, 2)), jnp.transpose(crossings, (1, 0, 2)), box_size,
       jnp.asarray(fwd), jnp.asarray(inv))
     divisor = (n * frames - jnp.arange(LAGS, dtype=jnp.int32)).astype(F32)

time: 24.5 us -> 22.6 us (0.922); the launches traced: 24.1 us -> 22.5 us
  Pallas kernels: 22.7 us -> 21.2 us
  other arithmetic: 1.31 us -> 0.61 us
  local copies, waits for them, and re-layouts: 0 us -> 0.65 us
    pallas_call x1, Pallas kernels: 22.7 us -> 21.2 us  [on_device(): pl.pallas_call(functools.partial(kernel, n), out_shape=jax.ShapeDtypeStru...]
    div x1, other arithmetic: 1.3 us -> 0.61 us  [on_device(): return lag_sum / divisor[None, :]]
    unnamed x0 -> x2, local copies, waits for them, and re-layouts: none -> 0.65 us
where the time goes in v2:
time: 22.6 us; the launch traced here: 22.5 us
  Pallas kernels  21.2 us (94%)
  local copies, waits for them, and re-layouts  0.65 us (3%)
  other arithmetic  0.61 us (3%)
    pallas_call x1, Pallas kernels, on_device(): pl.pallas_call(functools.partial(kernel, n), out_shape=jax.ShapeDtypeStru...  21.2 us
    unnamed x2, local copies, waits for them, and re-layouts  0.65 us
    div x1, other arithmetic, on_device(): return lag_sum / divisor[None, :]  0.61 us

profile of v2, /device:TPU:0, one launch (start us, length us, event | category | flops | bytes accessed | tf_op | source)
XLA Modules:
  0.0 22.5 jit_solution(2676614491034910772)
XLA Ops:
  0.0 0.0 copy-start
  0.0 0.6 %copy-done = f32[3]{0:T(128)S(1)} copy-done((f32[3]{0:T(128)S(1)}, f32[3]{0:T(128)}, u32[]{:S(2)}) %copy-start) | copy-done | bytes 36
  0.7 21.2 %shard_map.55 = f32[16,128]{1,0:T(8,128)S(1)} custom-call(f32[3,128,512]{2,1,0:T(8,128)} %bitcast.2, s32[3,128,512]{2,1,0:T(8,128)} %bitcast.3, f32[3]{0:T(128)S(1)} %copy-done, bf16[256,384]{1,0:T(8,128)(2,1)} %constant.6.clone.fwd_hbm, bf16[128,1280]{1,0:T(8,128)(2,1)} %constant.7.clone.inv_hbm), custom_call_target="tpu_custom_call" | custom-call | tf_op jit(solution)/shard_map/pallas_call | solution.py:387
  21.9 0.6 %broadcast_divide_fusion = f32[16,128]{1,0:T(8,128)} fusion(f32[16,128]{1,0:T(8,128)S(1)} %shard_map.55, f32[128]{0:T(128)S(1)} %subtract_convert_fusion), kind=kLoop, calls=%fused_computation | loop fusion | flops 2048 | bytes 16896 | tf_op jit(solution)/shard_map/div | solution.py:423
  (1 shorter events, 0.0 us)
Async XLA Ops:
  0.0 0.7 %copy-start = (f32[3]{0:T(128)S(1)}, f32[3]{0:T(128)}, u32[]{:S(2)}) copy-start(f32[3]{0:T(128)} %box_hbm.1) | copy-start | bytes 40

commit v3 on v2

--- a/solution.py
+++ b/solution.py
@@ -416,9 +416,10 @@
             pltpu.SemaphoreType.REGULAR,
             pltpu.SemaphoreType.REGULAR,
         ],
-        compiler_params=pltpu.CompilerParams(collective_id=0, has_side_effects=True, vmem_limit_bytes=55200*1024),
-    )(jnp.transpose(wrapped, (1, 0, 2)), jnp.transpose(crossings, (1, 0, 2)), box_size,
-      jnp.asarray(fwd), jnp.asarray(inv))
+        compiler_params=pltpu.CompilerParams(collective_id=0, has_side_effects=True, vmem_limit_bytes=32 * 2**20),
+    )(*(pltpu.with_memory_space_constraint(v, pltpu.HBM) for v in (
+        jnp.transpose(wrapped, (1, 0, 2)), jnp.transpose(crossings, (1, 0, 2)), box_size,
+        jnp.asarray(fwd), jnp.asarray(inv))))
     divisor = (n * frames - jnp.arange(LAGS, dtype=jnp.int32)).astype(F32)
     return lag_sum / divisor[None, :]
 

time: 22.6 us -> 22 us (0.973)
  local copies, waits for them, and re-layouts: 0.65 us -> 0 us
    unnamed x2 -> x0, local copies, waits for them, and re-layouts: 0.65 us -> none
where the time goes in v3:
time: 22 us; the launch traced here: 21.9 us
  Pallas kernels  21.2 us (96%)
  other arithmetic  0.61 us (3%)
    pallas_call x1, Pallas kernels, on_device(): pl.pallas_call(functools.partial(kernel, n), out_shape=jax.ShapeDtypeStru...  21.2 us
    div x1, other arithmetic, on_device(): return lag_sum / divisor[None, :]  0.61 us

profile of v3, /device:TPU:0, one launch (start us, length us, event | category | flops | bytes accessed | tf_op | source)
XLA Modules:
  0.0 21.9 jit_solution(10424468756267073538)
XLA Ops:
  0.0 21.2 %shard_map.55 = f32[16,128]{1,0:T(8,128)S(1)} custom-call(f32[3,128,512]{2,1,0:T(8,128)} %bitcast.2, s32[3,128,512]{2,1,0:T(8,128)} %bitcast.3, f32[3]{0:T(128)} %box_hbm.1, bf16[256,384]{1,0:T(8,128)(2,1)} %constant.6.clone.fwd_hbm, bf16[128,1280]{1,0:T(8,128)(2,1)} %constant.7.clone.inv_hbm), custom_call_target="tpu_custom_call" | custom-call | tf_op jit(solution)/shard_map/pallas_call | solution.py:387
  21.2 0.6 %broadcast_divide_fusion = f32[16,128]{1,0:T(8,128)} fusion(f32[16,128]{1,0:T(8,128)S(1)} %shard_map.55, f32[128]{0:T(128)S(1)} %subtract_convert_fusion), kind=kLoop, calls=%fused_computation | loop fusion | flops 2048 | bytes 16896 | tf_op jit(solution)/shard_map/div | solution.py:424
  (1 shorter events, 0.0 us)

commit v4 on v3

--- a/solution.py
+++ b/solution.py
@@ -105,8 +105,6 @@
     const_copies = [pltpu.make_async_copy(fwd_hbm, fwd, const_sem.at[0]),
                     pltpu.make_async_copy(inv_hbm, inv, const_sem.at[1]),
                     pltpu.make_async_copy(box_hbm, box, const_sem.at[2])]
-    for copy in const_copies:
-        copy.start()
 
     lane = lax.broadcasted_iota(jnp.int32, (SUB, LANES), 1)
     sub = lax.broadcasted_iota(jnp.int32, (SUB, LANES), 0)
@@ -170,10 +168,18 @@
             pl.semaphore_wait(barrier, greeted)
             signal(diag_sem, nearby(1, core))
 
-        exchange(c, 1)[1].start()
-
-        if c == 2:
-            exchange(c, 3)[1].start()
+        if c < 2:
+            exchange(c, 1)[1].start()
+        else:
+            @pl.when(chip == SLOTS - 1)
+            def _():
+                exchange(2, 3)[1].start()
+                exchange(2, 1)[1].start()
+
+            @pl.when(chip != SLOTS - 1)
+            def _():
+                exchange(2, 1)[1].start()
+                exchange(2, 3)[1].start()
 
         exchange(c, 2)[1].start()
         mine, remote, local = exchange(c, 0)
@@ -186,6 +192,9 @@
         def _():
             remote.start()
 
+        if c == 0:
+            for copy in const_copies:
+                copy.start()
         if c == 1:
             pl.semaphore_wait(diag_sem, 1)
             exchange(0, 3)[1].start()
@@ -218,12 +227,19 @@
 
     offs = {}
 
+    direct = jnp.logical_and(x == 0, y == 1)
+
+    def take_first(c):
+        landed(0, c)
+
+        @pl.when(quad > 0)
+        def _():
+            hand_on(c).start()
+
     def arrive(c):
-        landed(0, c)
-
-        @pl.when(quad > 0)
-        def _():
-            hand_on(c).start()
+        @pl.when(jnp.logical_not(direct))
+        def _():
+            take_first(c)
 
         for s in range(1, SLOTS):
             landed(s, c)
@@ -300,6 +316,11 @@
     @pl.when(is_last)
     def _():
         halo_sq[...] = jnp.zeros_like(halo_sq)
+
+    @pl.when(direct)
+    def _():
+        for c in range(dims):
+            take_first(c)
 
     arrive(0)
     spread(0, rounds)

time: 22 us -> 21.9 us (level); the launches traced: 21.9 us -> 21.5 us
  Pallas kernels: 21.2 us -> 20.9 us
    pallas_call x1, Pallas kernels: 21.2 us -> 20.9 us  [on_device(): pl.pallas_call(functools.partial(kernel, n), out_shape=jax.ShapeDtypeStru...]
where the time goes in v4:
time: 21.9 us; the launch traced here: 21.5 us
  Pallas kernels  20.9 us (95%)
  other arithmetic  0.61 us (3%)
    pallas_call x1, Pallas kernels, on_device(): pl.pallas_call(functools.partial(kernel, n), out_shape=jax.ShapeDtypeStru...  20.9 us
    div x1, other arithmetic, on_device(): return lag_sum / divisor[None, :]  0.61 us

profile of v4, /device:TPU:0, one launch (start us, length us, event | category | flops | bytes accessed | tf_op | source)
XLA Modules:
  0.0 21.5 jit_solution(10886654944891035122)
XLA Ops:
  0.0 20.9 %shard_map.55 = f32[16,128]{1,0:T(8,128)S(1)} custom-call(f32[3,128,512]{2,1,0:T(8,128)} %bitcast.2, s32[3,128,512]{2,1,0:T(8,128)} %bitcast.3, f32[3]{0:T(128)} %box_hbm.1, bf16[256,384]{1,0:T(8,128)(2,1)} %constant.6.clone.fwd_hbm, bf16[128,1280]{1,0:T(8,128)(2,1)} %constant.7.clone.inv_hbm), custom_call_target="tpu_custom_call" | custom-call | tf_op jit(solution)/shard_map/pallas_call | solution.py:408
  20.9 0.6 %broadcast_divide_fusion = f32[16,128]{1,0:T(8,128)} fusion(f32[16,128]{1,0:T(8,128)S(1)} %shard_map.55, f32[128]{0:T(128)S(1)} %subtract_convert_fusion), kind=kLoop, calls=%fused_computation | loop fusion | flops 2048 | bytes 16896 | tf_op jit(solution)/shard_map/div | solution.py:445
  (1 shorter events, 0.0 us)
